TPU v7x, 512 devices: a whole 4x8x8 slice. The times are simulated.
512 devices in a mesh: seq: 64 (over z, x, core), head: 8 (over y).
Axes of the slice: x: 4, y: 8, z: 8, core: 2. Of those that a mesh axis runs over, the one named last changes fastest.
Arguments:
- xbc: bfloat16 [24576, 10240], P('seq', 'head'), may hold values from -6 to 6
- gate_z: bfloat16 [24576, 8192], P('seq', 'head'), may hold values from -6 to 6
- dt_raw: bfloat16 [128, 24576], P('head', 'seq'), may hold values from -3 to 3
- dt_bias: float32 [128], P('head'), may hold values from -1 to 0.5
- a_log: float32 [128], P('head'), may hold values from -11.5 to -6.6
- skip_d: float32 [128], P('head'), may hold values from 0.5 to 1.5
- conv_weight: float32 [4, 10240], P(None, 'head'), may hold values from -3 to 3
- conv_bias: float32 [10240], P('head'), may hold values from -3 to 3
- norm_gain: float32 [8192], P('head'), may hold values from 0.1 to 1.9
- out_weight: bfloat16 [8192, 4096], P('head', 'seq'), may hold values from -0.1875 to 0.1875
- starts: int32 [24576], P('seq'), may hold values from 0 to 1, as said below
Outputs:
- mixed: bfloat16 [24576, 4096], P('seq', 'head')
Inputs may be any that keep to these rules, and one draw needn't show every extreme that they name: `starts`: a 0 or 1 flag for every token; every 1 lies among the first 6144 tokens, and there is at least one.
All inputs are finite; a program needn't handle non-finite values.
Results may differ from a plain program's by a relative error of at most 0.013.
Values may be sent and summed in bfloat16 or wider, within the bound.
A program may use at most 128 MiB of HBM per device.

v0:
```python
import jax
import jax.numpy as jnp
from jax import lax
from jax.sharding import PartitionSpec as P

P_SIZE = 64
N = 128
DI = 8192
HG = 16
GW = 1280


def carried_in(part, axis, combine, identity):
    place = lax.axis_index(axis)
    gathered = jax.tree.map(lambda a: lax.all_gather(a, axis), part)
    state = jax.tree.map(lambda a, e: jnp.zeros_like(a) + jnp.asarray(e, a.dtype), part, identity)

    def one(hop, state):
        return combine(
            state, jax.tree.map(lambda a: lax.dynamic_index_in_dim(a, hop, 0, False), gathered)
        )

    return lax.fori_loop(0, place, one, state)


def passed_along(block, axis, distance):
    devices = range(lax.axis_size(axis))
    route = [(i - distance, i) for i in devices if i - distance in devices]
    return lax.ppermute(block, axis, route)


def combine(earlier, later):
    return (earlier[0] * later[0], later[0][:, None, None] * earlier[1] + later[1])


def chain_states(decays, states):
    identity = (jnp.ones_like(decays), jnp.zeros_like(states))
    result = carried_in((decays, states), "seq", combine, identity)
    return result[1]


def block_local(item):
    xc, bc, cc, dtc, lc, sc = item
    cumul = jnp.cumsum(lc, axis=1)
    runs = jnp.cumsum(sc)
    tail = (
        jnp.where(
            (runs == runs[-1])[None, :], jnp.exp(jnp.minimum(cumul[:, -1:] - cumul, 0.0)), 0.0
        )
        * dtc
    )
    b_heads = jnp.repeat(bc, HG, axis=1)
    scaled = (tail[:, :, None] * jnp.swapaxes(b_heads, 0, 1).astype(jnp.float32)).astype(
        jnp.bfloat16
    )
    local = jnp.einsum("shp,hsn->hpn", xc, scaled, preferred_element_type=jnp.float32)
    total = jnp.exp(cumul[:, -1]) * (runs[-1] == 0).astype(jnp.float32)
    enter = jnp.exp(cumul) * (runs == 0).astype(jnp.float32)[None, :]
    return (local, total, enter)


def block_inner(item):
    xc, bc, cc, dtc, lc, sc = item
    length = xc.shape[0]
    cumul = jnp.cumsum(lc, axis=1)
    runs = jnp.cumsum(sc)
    lower = jnp.arange(length)[:, None] >= jnp.arange(length)[None, :]
    same = lower & (runs[:, None] == runs[None, :])
    diff = cumul[:, :, None] - cumul[:, None, :]
    wdec = jnp.where(same[None], jnp.exp(jnp.minimum(diff, 0.0)), 0.0)
    scores = jnp.einsum("tgn,sgn->gts", cc, bc, preferred_element_type=jnp.float32)
    scores_h = jnp.repeat(scores, HG, axis=0)
    weights = (scores_h * wdec * dtc[:, None, :]).astype(jnp.bfloat16)
    return jnp.einsum("hts,shp->thp", weights, xc, preferred_element_type=jnp.float32)


def body(
    xbc,
    gate_z,
    dt_raw,
    dt_bias,
    a_log,
    skip_d,
    conv_weight,
    conv_bias,
    norm_gain,
    out_weight,
    starts,
):
    tok = xbc.shape[0]
    width = conv_weight.shape[0]
    chans = xbc.shape[1]
    groups = chans // GW
    heads = dt_raw.shape[0]
    rim, rim_flags = passed_along(
        (xbc[tok - (width - 1) :], starts[tok - (width - 1) :].astype(jnp.bfloat16)), "seq", 1
    )
    flags_int = rim_flags.astype(jnp.int32)
    after_rim = jnp.sum(flags_int) - jnp.cumsum(flags_int)
    counts = jnp.cumsum(starts)
    padded = jnp.concatenate([rim, xbc], axis=0).astype(jnp.float32)
    count_ext = jnp.concatenate([-after_rim, counts])
    acc = conv_bias[None, :] + conv_weight[width - 1][None, :] * xbc.astype(jnp.float32)
    for lag in range(1, width):
        shifted = padded[width - 1 - lag : width - 1 - lag + tok]
        keep = (count_ext[width - 1 - lag : width - 1 - lag + tok] == counts).astype(jnp.float32)
        acc = acc + conv_weight[width - 1 - lag][None, :] * shifted * keep[:, None]
    unit = jax.nn.silu(acc).astype(jnp.bfloat16)
    grid = unit.reshape(tok, groups, GW)
    xs = grid[:, :, : HG * P_SIZE].reshape(tok, heads, P_SIZE)
    bmat = grid[:, :, HG * P_SIZE : HG * P_SIZE + N]
    cmat = grid[:, :, HG * P_SIZE + N :]
    steps_dt = jax.nn.softplus(dt_raw.astype(jnp.float32) + dt_bias[:, None])
    logs = -jnp.exp(a_log)[:, None] * steps_dt
    length = min(128, tok)
    nblocks = tok // length
    x_blocks = xs.reshape(nblocks, length, heads, P_SIZE)
    b_blocks = bmat.reshape(nblocks, length, groups, N)
    c_blocks = cmat.reshape(nblocks, length, groups, N)
    dt_blocks = steps_dt.reshape(heads, nblocks, length).transpose(1, 0, 2)
    log_blocks = logs.reshape(heads, nblocks, length).transpose(1, 0, 2)
    start_blocks = starts.reshape(nblocks, length)
    items = (x_blocks, b_blocks, c_blocks, dt_blocks, log_blocks, start_blocks)

    def fold(carry, item):
        local, total = item
        return ((carry[0] * total, carry[1] * total[:, None, None] + local), None)

    y_diag, (locals_all, totals, enters) = lax.map(
        lambda item: (block_inner(item), block_local(item)), items
    )
    init = (jnp.ones((heads,), jnp.float32), jnp.zeros((heads, P_SIZE, N), jnp.float32))
    result, unused = lax.scan(fold, init, (locals_all, totals))
    entering = chain_states(result[0], result[1])

    def apply(state, item):
        cc, enter, local, total = item
        c_heads = jnp.repeat(cc, HG, axis=1)
        y_off = (
            jnp.einsum(
                "thn,hpn->thp",
                c_heads,
                state.astype(jnp.bfloat16),
                preferred_element_type=jnp.float32,
            )
            * enter.T[:, :, None]
        )
        return (state * total[:, None, None] + local, y_off)

    unused_state, y_offs = lax.scan(apply, entering, (c_blocks, enters, locals_all, totals))
    y_all = (y_diag + y_offs).reshape(tok, heads, P_SIZE) + skip_d[None, :, None] * xs.astype(
        jnp.float32
    )
    gated = y_all.reshape(tok, heads * P_SIZE) * jax.nn.silu(gate_z.astype(jnp.float32))
    total_sq = lax.psum(jnp.sum(gated * gated, axis=1), "head")
    normed = (gated * lax.rsqrt(total_sq / DI + 1e-05)[:, None] * norm_gain[None, :]).astype(
        jnp.bfloat16
    )
    terms = jnp.dot(
        normed,
        lax.all_gather(out_weight, "seq", axis=1, tiled=True),
        preferred_element_type=jnp.float32,
    )
    return lax.psum_scatter(terms.astype(jnp.bfloat16), "head", scatter_dimension=1, tiled=True)


def solution(mesh):
    placed = (
        P("seq", "head"),
        P("seq", "head"),
        P("head", "seq"),
        P("head"),
        P("head"),
        P("head"),
        P(None, "head"),
        P("head"),
        P("head"),
        P("head", "seq"),
        P("seq"),
    )
    return jax.shard_map(
        body, mesh=mesh, in_specs=placed, out_specs=P("seq", "head"), check_vma=False
    )
```

profile of v0, /device:TPU:2, one launch (start us, length us, event | category | flops | bytes accessed | tf_op | source)
XLA Modules:
  0.0 368.8 jit_solution(15041050396364430548)
XLA Ops:
  6.5 0.7 convert.4
  7.3 1.9 collective-permute-start.1
  9.2 0.7 slice.66
  10.0 3.5 collective-permute-start
  13.5 1.0 reduce-window.22
  14.8 0.9 slice_reduce_fusion.4
  15.7 0.7 exponential_negate_fusion
  16.4 0.8 compare_select_fusion
  17.5 0.7 convert_reduce_fusion
  18.2 0.7 negate_bitcast_fusion
  19.0 1.4 maximum_convert_fusion
  20.5 1.9 fusion.44
  22.4 0.9 copy-done.1
  23.3 1.9 reshape.277
  25.2 2.0 copy.38
  27.2 1.3 broadcast.139.clone
  28.5 17.6 %while.53 = (s32[]{:T(128)}, f32[3,128,16,64]{1,3,2,0:T(8,128)}, f32[3,16,64,128]{3,2,1,0:T(8,128)S(1)}, f32[3,16]{1,0:T(4,128)S(1)}, f32[3,16,128]{2,1,0:T(8,12...) while((s32[]{:T(128)}, f32[3,128,16,64]{1,3,2,0:T(8,128)}, ...), condition=%wide.region_7.8_spmd, body=%wide.region_4.7_spmd.sunk | while | flops 73752848 | bytes 2099011 | solution.py:129
  28.9 0.7 fusion.73
  29.8 0.6 slice.143
  31.4 0.7 compare_convert_fusion.2
  33.0 1.4 fusion.75
  34.7 0.7 fusion.73
  37.3 0.7 compare_convert_fusion.2
  38.9 1.4 fusion.75
  40.6 0.7 fusion.73
  43.2 0.7 compare_convert_fusion.2
  44.7 1.4 fusion.75
  46.7 0.8 copy-done
  47.5 0.7 all-gather.5.cloned.1.call-update
  48.4 1.3 dynamic-slice
  50.7 130.2 %all-reduce = f32[1024]{0:T(1024)S(1)} all-reduce(f32[1024]{0:T(1024)S(1)} %dynamic-update-slice), channel_id=2, replica_groups=mesh['seq'=64,'head'=8] {'seq'}, use_global_device_ids=true, to_apply=%add | all-reduce | flops 1024 | bytes 8192
  181.0 18.2 %all-gather.7.cloned.1.call-done = f32[1024,64,128]{2,1,0:T(8,128)} async-done(((f32[16,64,128]{2,1,0:T(8,128)}), f32[1024,64,128]{2,1,0:T(8,128)}) %all-gather.7.cloned.1.call-update) | async-done | bytes 33554448 | tf_op jit(solution)/shard_map/all_gather | solution.py:15
  199.3 2.5 while.54
  199.3 1.2 bitcast_add_fusion.6
  200.5 1.2 bitcast_add_fusion.6
  201.7 1.3 broadcast.139
  203.1 4.4 %while.55 = (s32[]{:T(128)}, f32[16,64,128]{2,1,0:T(8,128)S(1)}, f32[3,128,16,64]{1,3,2,0:T(8,128)}, f32[3,16]{1,0:T(4,128)S(1)}, f32[3,16,64,128]{3,2,1,0:T(8,1...) while((s32[]{:T(128)}, f32[16,64,128]{2,1,0:T(8,128)S(1)}, ...), condition=%wide.region_13.14_spmd, body=%wide.region_12.13_spmd.sunk | while | flops 34078720 | bytes 2745125 | solution.py:150
  203.1 1.3 fusion.81
  204.6 1.3 fusion.81
  206.0 1.3 fusion.81
  207.5 3.4 add.93
  210.9 2.3 copy.48
  213.2 1.8 reshape.278
  215.0 2.6 multiply_reduce_fusion.1
  217.6 17.0 %psum.7 = f32[384]{0:T(512)S(1)} all-reduce(f32[384]{0:T(512)S(1)} %get-tuple-element.329), channel_id=1, replica_groups=mesh['seq'=64,'head'=8] {'head'}, use_global_device_ids=true, to_apply=%region_15.16 | all-reduce | flops 384 | bytes 3072 | tf_op jit(solution)/shard_map/psum | solution.py:155
  234.6 53.6 %all-gather.5.cloned.1.call-done = bf16[1024,4096]{0,1:T(8,128)(2,1)} async-done(((bf16[1024,64]{0,1:T(8,128)(2,1)}), bf16[1024,4096]{0,1:T(8,128)(2,1)}) %all-gather.5.cloned.1.call-update) | async-done | bytes 8388624 | tf_op jit(solution)/shard_map/all_gather | solution.py:161
  288.3 10.2 %convolution_convert_fusion = bf16[384,4096]{1,0:T(8,128)(2,1)} fusion(bf16[1024,4096]{0,1:T(8,128)(2,1)} %all-gather.5.cloned.1.call-done, f32[384,1024]{1,0:T(8,128)S(1)} %get-tuple-element.330, f32[1024]{0:T(1024)S(1)} %copy-done.5, f32[384]{0:T(512)S(1)} %add_rsqrt_fusion), kind=kOutput, calls=%fused_computation.59 | convolution fusion | flops 3223977984 | bytes 13112832 | tf_op jit(solution)/shard_map/dot_general | solution.py:159
  298.5 63.8 %reduce-scatter.2.cloned.1.call-done = bf16[384,512]{1,0:T(8,128)(2,1)} async-done(((bf16[384,4096]{1,0:T(8,128)(2,1)}), bf16[384,512]{1,0:T(8,128)(2,1)}) %reduce-scatter.2.cloned.1.call-update) | async-done | bytes 393232 | tf_op jit(solution)/shard_map/reduce_scatter | solution.py:164
  (104 shorter events, 9.4 us)
Async XLA Ops:
  6.5 192.7 %all-gather.7.cloned.1.call-start = ((), (), s32[]{:S(2)}) async-start(), calls=%async_computation.3 | async-start | bytes 34078720 | tf_op jit(solution)/shard_map/all_gather | solution.py:15
  7.3 10.0 %collective-permute-start.1 = (bf16[3]{0:T(256)(128)(2,1)S(1)}, bf16[3]{0:T(256)(128)(2,1)S(1)}, u32[]{:S(2)}, u32[]{:S(2)}) collective-permute-start(bf16[3]{0:T(256)(128)(2,1)S(1)} %slice.68), channel_id=1, source_target_pairs={{0,8},{8,16},{16,24},{24,32},{32,40},{40,48},{48,56},{56,64},{64,7... | collective-permute-start | bytes 26 | tf_op jit(solution)/shard_map/ppermute | solution.py:29
  10.0 9.1 %collective-permute-start = (bf16[3,1280]{1,0:T(4,128)(2,1)S(1)}, bf16[3,1280]{1,0:T(4,128)(2,1)S(1)}, u32[]{:S(2)}, u32[]{:S(2)}) collective-permute-start(bf16[3,1280]{1,0:T(4,128)(2,1)S(1)} %slice.66), channel_id=1, source_target_pairs={{0,8},{8,16},{16,24},{24,32},{32,40},{40,48},{48,56},{56,64},{64,7... | collective-permute-start | bytes 23048 | tf_op jit(solution)/shard_map/ppermute | solution.py:29
  17.2 3.2 copy-start.2
  17.2 3.2 copy-start.3
  22.3 1.0 copy-start.1
  46.1 2.1 copy-start.4
  46.6 0.8 copy-start
  47.5 240.8 %all-gather.5.cloned.1.call-start = ((), (), s32[]{:S(2)}) async-start(), calls=%async_computation.1 | async-start | bytes 8519680 | tf_op jit(solution)/shard_map/all_gather | solution.py:161
  48.2 314.0 %reduce-scatter.2.cloned.1.call-start = ((), (), s32[]{:S(2)}) async-start(), calls=%async_computation.2 | async-start | bytes 3538944 | tf_op jit(solution)/shard_map/reduce_scatter | solution.py:164
  215.0 73.2 %copy-start.5 = (f32[1024]{0:T(1024)S(1)}, f32[1024]{0:T(1024)}, u32[]{:S(2)}) copy-start(f32[1024]{0:T(1024)} %param.27) | copy-start | bytes 12292
Sparse Core Ops, SparseCore 0:
  47.6 151.5 all-gather.6
  202.6 85.6 all-gather.4
  298.6 63.6 reduce-scatter.1
where the time goes:
time: 372 us; the launch traced here: 369 us
  blocking collectives  147 us (40%)
  waiting for transfers between devices  136 us (37%)
  other arithmetic  22.4 us (6%)
  local copies, waits for them, and re-layouts  20.7 us (6%)
  matrix products  20.1 us (5%)
  between operations  14 us (4%)
  starting transfers between devices  5.48 us (1%)
    unnamed x1, blocking collectives  130 us
    reduce_scatter x1, waiting for transfers between devices, body(): lax.psum_scatter(terms.astype(jnp.bfloat16), 'head', scatter_dimension=1,...  63.8 us
    all_gather x1, waiting for transfers between devices, body(): lax.all_gather(out_weight, 'seq', axis=1, tiled=True)  53.6 us
    all_gather x1, waiting for transfers between devices, carried_in(): gathered = jax.tree.map(lambda a: lax.all_gather(a, axis), part)  18.2 us
    psum x1, blocking collectives, body(): total_sq = lax.psum(jnp.sum(gated * gated, axis=1), 'head')  17 us
    dot_general x1, matrix products, body(): jnp.dot(normed, lax.all_gather(out_weight, 'seq', axis=1, tiled=True), pr...  10.2 us
  transfers between devices with their start and end apart: 5, of which 3 were waited for; matrix products, arithmetic and copies ran while one was open for 7% of the time, Pallas kernels for 0%

commit v1 on v0

--- a/solution.py
+++ b/solution.py
@@ -158,7 +158,9 @@
     )
     terms = jnp.dot(
         normed,
-        lax.all_gather(out_weight, "seq", axis=1, tiled=True),
+        jnp.concatenate(
+            lax.all_to_all(jnp.stack([out_weight] * lax.axis_size("seq")), "seq", 0, 0), axis=1
+        ),
         preferred_element_type=jnp.float32,
     )
     return lax.psum_scatter(terms.astype(jnp.bfloat16), "head", scatter_dimension=1, tiled=True)

time: 372 us -> 593 us (1.59)
  the two profiles are of different devices: /device:TPU:2 before, /device:TPU:6 now
where the time goes in v1:
time: 593 us; the launch traced here: 589 us
  blocking collectives  365 us (62%)
  waiting for transfers between devices  116 us (20%)
  other arithmetic  27.1 us (5%)
  local copies, waits for them, and re-layouts  24.9 us (4%)
  matrix products  20.1 us (3%)
  starting transfers between devices  19.3 us (3%)
  between operations  14.3 us (2%)
    unnamed x1, blocking collectives  347 us
    reduce_scatter x1, waiting for transfers between devices, body(): lax.psum_scatter(terms.astype(jnp.bfloat16), 'head', scatter_dimension=1,...  116 us
    psum x1, blocking collectives, body(): total_sq = lax.psum(jnp.sum(gated * gated, axis=1), 'head')  17.8 us
    all_to_all x1, starting transfers between devices, body(): lax.all_to_all(jnp.stack([out_weight] * lax.axis_size('seq')), 'seq', 0, 0)  13 us
  transfers between devices with their start and end apart: 5, of which 1 were waited for; matrix products, arithmetic and copies ran while one was open for 6% of the time, Pallas kernels for 0%

profile of v1, /device:TPU:6, one launch (start us, length us, event | category | flops | bytes accessed | tf_op | source)
XLA Modules:
  0.0 589.3 jit_solution(7239803485912360249)
XLA Ops:
  7.3 1.9 collective-permute-start.1
  9.2 0.7 slice.66
  10.0 4.3 collective-permute-start
  14.3 1.0 reduce-window.22
  15.6 0.9 slice_reduce_fusion.4
  17.2 0.8 compare_select_fusion
  18.3 0.7 convert_reduce_fusion
  19.0 0.7 negate_bitcast_fusion
  19.8 1.4 maximum_convert_fusion
  21.3 1.9 fusion.44
  23.2 0.8 copy-done.1
  24.1 1.9 reshape.287
  26.0 2.0 copy.39
  28.0 1.3 broadcast.141.clone
  29.3 17.6 %while.53 = (s32[]{:T(128)}, f32[3,128,16,64]{1,3,2,0:T(8,128)}, f32[3,16,64,128]{3,2,1,0:T(8,128)S(1)}, f32[3,16]{1,0:T(4,128)S(1)}, f32[3,16,128]{2,1,0:T(8,12...) while((s32[]{:T(128)}, f32[3,128,16,64]{1,3,2,0:T(8,128)}, ...), condition=%wide.region_7.8_spmd, body=%wide.region_4.7_spmd.sunk | while | flops 73752848 | bytes 2099011 | solution.py:129
  29.6 0.7 fusion.73
  32.2 0.7 compare_convert_fusion.2
  33.8 1.4 fusion.75
  35.5 0.7 fusion.73
  38.1 0.7 compare_convert_fusion.2
  39.6 1.4 fusion.75
  41.4 0.7 fusion.73
  43.9 0.7 compare_convert_fusion.2
  45.5 1.4 fusion.75
  47.4 0.8 copy-done
  48.2 4.3 stack.2
  52.5 13.0 %all-to-all-start = ((bf16[64,1024,64]{1,2,0:T(8,128)(2,1)}), bf16[64,1024,64]{1,2,0:T(8,128)(2,1)}, u32[]{:S(2)}, u32[]{:S(2)}) async-start(bf16[64,1024,64]{1,2,0:T(8,128)(2,1)} %stack.2), calls=%async_computation | async-start | bytes 16777216 | tf_op jit(solution)/shard_map/all_to_all | solution.py:162
  65.8 1.3 dynamic-slice
  67.9 347.1 %all-reduce = f32[1024]{0:T(1024)S(1)} all-reduce(f32[1024]{0:T(1024)S(1)} %dynamic-update-slice), channel_id=2, replica_groups=mesh['seq'=64,'head'=8] {'seq'}, use_global_device_ids=true, to_apply=%add | all-reduce | flops 1024 | bytes 8192
  415.2 7.4 %while.54 = (s32[]{:T(128)}, f32[16,64,128]{2,1,0:T(8,128)S(1)}, s32[]{:T(128)}, f32[64,16]{1,0:T(8,128)S(1)}, f32[64,16,64,128]{3,2,1,0:T(8,128)}, /*index=5*/s32[]{:T(128)}, s32[]{:T(128)}, s32[]{:T(128)}) while((s32[]{:T(128)}, f32[16,64,128]{2,1,0:T(8,128)S(1)}, s32[]{:T(128)}, f32[64,16]{1,0:T(8,128)S(1)}, ...), condition=%wide.region_11.12_spmd, body=%wide.region_10.11_spmd.sunk | while | flops 262149 | bytes 1573183 | solution.py:23
  415.2 1.2 bitcast_add_fusion.6
  416.4 1.2 bitcast_add_fusion.6
  417.7 1.2 bitcast_add_fusion.6
  418.9 1.2 bitcast_add_fusion.6
  420.2 1.2 bitcast_add_fusion.6
  421.4 1.2 bitcast_add_fusion.6
  422.6 1.3 broadcast.141
  423.9 4.4 while.55
  423.9 1.3 fusion.81
  425.4 1.3 fusion.81
  426.9 1.3 fusion.81
  428.3 3.4 add.93
  431.7 2.3 copy.49
  434.0 1.8 reshape.288
  435.9 2.5 multiply_reduce_fusion.1
  438.4 17.8 %psum.7 = f32[384]{0:T(512)S(1)} all-reduce(f32[384]{0:T(512)S(1)} %get-tuple-element.329), channel_id=1, replica_groups=mesh['seq'=64,'head'=8] {'head'}, use_global_device_ids=true, to_apply=%region_15.16 | all-reduce | flops 384 | bytes 3072 | tf_op jit(solution)/shard_map/psum | solution.py:155
  456.2 10.2 %convolution_convert_fusion = bf16[384,4096]{1,0:T(8,128)(2,1)} fusion(bf16[1024,4096]{0,1:T(8,128)(2,1)} %bitcast.36, f32[384,1024]{1,0:T(8,128)S(1)} %get-tuple-element.330, f32[1024]{0:T(1024)S(1)} %copy-done.6, f32[384]{0:T(512)S(1)} %add_rsqrt_fusion), kind=kOutput, calls=%fused_computation.59 | convolution fusion | flops 3223977984 | bytes 13112832 | tf_op jit(solution)/shard_map/dot_general | solution.py:159
  466.4 116.0 %reduce-scatter.2.cloned.1.call-done = bf16[384,512]{1,0:T(8,128)(2,1)} async-done(((bf16[384,4096]{1,0:T(8,128)(2,1)}), bf16[384,512]{1,0:T(8,128)(2,1)}) %reduce-scatter.2.cloned.1.call-update) | async-done | bytes 393232 | tf_op jit(solution)/shard_map/reduce_scatter | solution.py:166
  (114 shorter events, 11.4 us)
Async XLA Ops:
  6.5 408.6 %all-gather.4.cloned.1.call-start = ((), (), s32[]{:S(2)}) async-start(), calls=%async_computation.3 | async-start | bytes 34078720 | tf_op jit(solution)/shard_map/all_gather | solution.py:15
  7.3 10.8 %collective-permute-start.1 = (bf16[3]{0:T(256)(128)(2,1)S(1)}, bf16[3]{0:T(256)(128)(2,1)S(1)}, u32[]{:S(2)}, u32[]{:S(2)}) collective-permute-start(bf16[3]{0:T(256)(128)(2,1)S(1)} %slice.68), channel_id=1, source_target_pairs={{0,8},{8,16},{16,24},{24,32},{32,40},{40,48},{48,56},{56,64},{64,7... | collective-permute-start | bytes 26 | tf_op jit(solution)/shard_map/ppermute | solution.py:29
  10.0 9.9 %collective-permute-start = (bf16[3,1280]{1,0:T(4,128)(2,1)S(1)}, bf16[3,1280]{1,0:T(4,128)(2,1)S(1)}, u32[]{:S(2)}, u32[]{:S(2)}) collective-permute-start(bf16[3,1280]{1,0:T(4,128)(2,1)S(1)} %slice.66), channel_id=1, source_target_pairs={{0,8},{8,16},{16,24},{24,32},{32,40},{40,48},{48,56},{56,64},{64,7... | collective-permute-start | bytes 23048 | tf_op jit(solution)/shard_map/ppermute | solution.py:29
  18.0 3.2 copy-start.2
  18.0 3.2 copy-start.4
  23.1 1.0 copy-start.1
  46.9 1.3 copy-start.3
  47.4 0.8 copy-start
  52.5 13.1 %copy-start.5 = (f32[16]{0:T(128)S(1)}, f32[16]{0:T(128)}, u32[]{:S(2)}) copy-start(f32[16]{0:T(128)} %param.24) | copy-start | bytes 196
  52.5 403.7 %all-to-all-start = ((bf16[64,1024,64]{1,2,0:T(8,128)(2,1)}), bf16[64,1024,64]{1,2,0:T(8,128)(2,1)}, u32[]{:S(2)}, u32[]{:S(2)}) async-start(bf16[64,1024,64]{1,2,0:T(8,128)(2,1)} %stack.2), calls=%async_computation | async-start | bytes 16777216 | tf_op jit(solution)/shard_map/all_to_all | solution.py:162
  65.5 516.9 %reduce-scatter.2.cloned.1.call-start = ((), (), s32[]{:S(2)}) async-start(), calls=%async_computation.2 | async-start | bytes 3538944 | tf_op jit(solution)/shard_map/reduce_scatter | solution.py:166
  435.9 20.3 %copy-start.6 = (f32[1024]{0:T(1024)S(1)}, f32[1024]{0:T(1024)}, u32[]{:S(2)}) copy-start(f32[1024]{0:T(1024)} %param.27) | copy-start | bytes 12292
Sparse Core Ops, SparseCore 0:
  48.3 302.0 all-gather.3
  466.5 115.8 reduce-scatter.1
